TPU v7x, 32 devices: a whole 2x2x4 slice. The times are simulated.
32 devices in a mesh: block: 4 (over y, x), tok: 8 (over z, core).
Axes of the slice: x: 2, y: 2, z: 4, core: 2. Of those that a mesh axis runs over, the one named last changes fastest.
Arguments:
- keys: bfloat16 [4, 2, 2048, 1280], P('block', None, 'tok'), may hold values from -6 to 6
- values: bfloat16 [4, 2, 2048, 1280], P('block', None, 'tok'), may hold values from -6 to 6
- queries: bfloat16 [4, 2, 2048, 1280], P('block', None, 'tok'), may hold values from -6 to 6
- rates: bfloat16 [4, 2, 2048, 20], P('block', None, 'tok'), may hold values from 0.00049972534 to 0.0049743652
- counts: int32 [4, 2, 8, 20], P('block', None, 'tok'), may hold values from 1 to 256
- stagger: int32 [20], replicated, may hold values from 0 to 255
- gate_in: bfloat16 [4, 20, 64, 512], P('block', None, None, 'tok'), may hold values from -0.75 to 0.75
- up_in: bfloat16 [4, 20, 64, 512], P('block', None, None, 'tok'), may hold values from -0.75 to 0.75
- down_in: bfloat16 [4, 20, 64, 512], P('block', None, None, 'tok'), may hold values from -0.25 to 0.25
- entry_gate: bfloat16 [20, 64, 512], replicated, may hold values from -0.75 to 0.75
- entry_up: bfloat16 [20, 64, 512], replicated, may hold values from -0.75 to 0.75
- entry_down: bfloat16 [20, 64, 512], replicated, may hold values from -0.25 to 0.25
Outputs:
- answers: bfloat16 [4, 2, 2048, 1280], P('block', None, 'tok')
- gate_out: bfloat16 [4, 20, 64, 512], P('block', None, None, 'tok')
- up_out: bfloat16 [4, 20, 64, 512], P('block', None, None, 'tok')
- down_out: bfloat16 [4, 20, 64, 512], P('block', None, None, 'tok')
All inputs are finite; a program needn't handle non-finite values.
Results may differ from a plain program's by a relative error of at most 0.022.
Values may be sent and summed in bfloat16 or wider, within the bound.
A program may use at most 320 MiB of HBM per device.

v0:
```python
import functools
import math

import jax
import jax.numpy as jnp
from jax import lax
from jax.experimental import pallas as pl
from jax.experimental.pallas import tpu as pltpu
from jax.sharding import PartitionSpec as P

EPS = 1e-06
F32 = jnp.float32
BF16 = jnp.bfloat16
MESH = pl.DeviceIdType.MESH


def row_scale(rates, counts, stagger):
    rows = rates.shape[1]
    offset = jnp.arange(rows, dtype=jnp.int32)[None, :, None]
    inside = jnp.mod(offset - stagger[None, None, :], rows)
    return jnp.where(inside < counts, rates, jnp.zeros_like(rates))


def sigmoid(x):
    return 0.5 * jnp.tanh(0.5 * x) + 0.5


def nn(a, b):
    return lax.dot_general(a, b, (((1,), (0,)), ((), ())), preferred_element_type=F32)


def nt(a, b):
    return lax.dot_general(a, b, (((1,), (1,)), ((), ())), preferred_element_type=F32)


def turned(x):
    return x.astype(F32).T.astype(BF16)


def kernel(
    groups, members, own, size, blocks,
    pack_ref, ask_ref, w_ref, entry_ref, ans_ref, wout_ref,
    kv, qs, full, carry, reply, acc, gut, wt, gut_all,
    kv_send, kv_recv, relay_send, relay_recv, q_send, q_recv,
    w_send, w_recv, carry_sem, a_send, a_recv, local,
):
    ticks = pack_ref.shape[0]
    edge = own * size
    hid = w_ref.shape[3]
    block = lax.axis_index("block")
    me = lax.axis_index("tok")
    z = me // members
    c = lax.rem(me, members)

    def behind(i):
        return lax.rem(z - i + groups, groups)

    def ahead(i):
        return lax.rem(z + i, groups)

    def mate(j):
        return lax.rem(c + j, members)

    def mate_back(j):
        return lax.rem(c - j + members, members)

    def at(zz, cc):
        return (block, zz * members + cc)

    def remote(src, dst, send, recv, device):
        return pltpu.make_async_remote_copy(
            src_ref=src, dst_ref=dst, send_sem=send, recv_sem=recv,
            device_id=device, device_id_type=MESH,
        )

    barrier = pltpu.get_barrier_semaphore()
    for i in range(1, groups):
        pl.semaphore_signal(barrier, inc=1, device_id=at(ahead(i), c), device_id_type=MESH)
    for j in range(1, members):
        pl.semaphore_signal(barrier, inc=1, device_id=at(z, mate(j)), device_id_type=MESH)

    @pl.when(block > 0)
    def _():
        pl.semaphore_signal(barrier, inc=1, device_id=(block - 1, me), device_id_type=MESH)

    @pl.when(block < blocks - 1)
    def _():
        pl.semaphore_signal(barrier, inc=1, device_id=(block + 1, me), device_id_type=MESH)

    near = jnp.where(block > 0, 1, 0) + jnp.where(block < blocks - 1, 1, 0)
    pl.semaphore_wait(barrier, groups - 1 + members - 1 + near)

    def kv_out(t, i):
        return remote(pack_ref.at[t, ahead(i)], kv.at[t, c, z], kv_send.at[t, i], kv_recv.at[t, i], at(ahead(i), c))

    def q_out(t, i):
        return remote(ask_ref.at[t, ahead(i)], qs.at[t, z], q_send.at[t, i], q_recv.at[t, i], at(ahead(i), c))

    def relay(t, j, i):
        part = kv.at[t, c, behind(i)]
        return remote(part, part, relay_send.at[t, j, i], relay_recv.at[t, j, i], at(z, mate(j)))

    def w_out(t, j):
        part = full.at[t, c]
        return remote(part, part, w_send.at[t, j], w_recv.at[t, j], at(z, mate(j)))

    def a_out(t, i):
        return remote(reply.at[t, behind(i)], ans_ref.at[t, z], a_send.at[t, i], a_recv.at[t, i], at(behind(i), c))

    def pass_on():
        return remote(full.at[0, c], carry, carry_sem.at[0], carry_sem.at[1], (lax.rem(block + 1, blocks), me))

    def kv_own(t):
        return pltpu.make_async_copy(pack_ref.at[t, z], kv.at[t, c, z], local.at[0, t])

    def q_own(t):
        return pltpu.make_async_copy(ask_ref.at[t, z], qs.at[t, z], local.at[1, t])

    def a_own(t):
        return pltpu.make_async_copy(reply.at[t, z], ans_ref.at[t, z], local.at[2, t])

    for i in range(1, groups):
        kv_out(0, i).start()
    for t in range(ticks):
        kv_own(t).start()
        q_own(t).start()

    for t in range(ticks):
        weights = w_ref if t == 0 else carry
        if t > 0:

            @pl.when(block == 0)
            def _():
                carry[...] = entry_ref[...]

            @pl.when(block > 0)
            def _():
                pass_on().wait_recv()

        for h in range(own):
            gut[h, :hid, :] = turned(weights[0, h])
            gut[h, hid:, :] = turned(weights[1, h])
            wt[h] = turned(weights[2, h])
        acc[...] = jnp.zeros_like(acc)
        kv_own(t).wait()

        def chunk(n, carried, t=t):
            j, i = n // groups, lax.rem(n, groups)

            @pl.when((j == 0) & (i > 0))
            def _():
                kv_out(t, i).wait_recv()

            @pl.when(j == 0)
            def _():
                for jj in range(1, members):
                    relay(t, jj, i).start()

            @pl.when(j > 0)
            def _():
                relay(t, j, i).wait_recv()

            part = kv.at[t, mate_back(j), behind(i)]
            scale = part[2 * edge :, :].astype(F32)
            for h in range(own):
                k = part[h * size : (h + 1) * size, :]
                v = part[edge + h * size : edge + (h + 1) * size, :]
                pre = nn(gut[h], k)
                back = nn(wt[h], v)
                gate, up = pre[:hid], pre[hid:]
                weight = scale[h : h + 1]
                sig = sigmoid(gate)
                act = gate * sig
                wb = weight * back
                hidden = (weight * act * up).astype(BF16)
                d_gate = (wb * up * (sig + act * (1.0 - sig))).astype(BF16)
                d_up = (wb * act).astype(BF16)
                acc[0, h] += nt(k, d_gate)
                acc[1, h] += nt(k, d_up)
                acc[2, h] += nt(v, hidden)
            return carried

        lax.fori_loop(0, groups, chunk, 0)
        if t == 0:
            for i in range(1, groups):
                q_out(0, i).start()
            for u in range(1, ticks):
                for i in range(1, groups):
                    kv_out(u, i).start()
                for i in range(1, groups):
                    q_out(u, i).start()
        lax.fori_loop(groups, groups * members, chunk, 0)

        for h in range(own):
            for p in range(3):
                base = weights[p, h].astype(F32)
                moved = base + acc[p, h]
                before = jnp.sum(base * base, axis=0, keepdims=True) + EPS
                after = jnp.sum(moved * moved, axis=0, keepdims=True) + EPS
                full[t, c, p, h] = (moved * (jnp.sqrt(before) / jnp.sqrt(after))).astype(BF16)
        for j in range(1, members):
            w_out(t, j).start()
        if t + 1 < ticks:

            @pl.when(block < blocks - 1)
            def _():
                pass_on().start()

        else:
            wout_ref[...] = full[t, c]
        for j in range(1, members):
            w_out(t, j).wait_recv()

        def prepare(s, carried, t=t):
            for h in range(own):
                gut_all[s, h, :hid, :] = turned(full[t, s, 0, h])
                gut_all[s, h, hid:, :] = turned(full[t, s, 1, h])
            return carried

        lax.fori_loop(0, members, prepare, 0)
        q_own(t).wait()

        def answer(n, carried, t=t):
            i = lax.rem(n + 1, groups)

            @pl.when(i > 0)
            def _():
                q_out(t, i).wait_recv()

            for h in range(own):
                q = qs[t, behind(i), h * size : (h + 1) * size, :]
                total = None
                for s in range(members):
                    pre = nn(gut_all[s, h], q)
                    gate, up = pre[:hid], pre[hid:]
                    hidden = (gate * sigmoid(gate) * up).astype(BF16)
                    term = nn(full[t, s, 2, h], hidden)
                    total = term if total is None else total + term
                reply[t, behind(i), h * size : (h + 1) * size, :] = total.astype(BF16)

            @pl.when(i > 0)
            def _():
                a_out(t, i).start()

            return carried

        lax.fori_loop(0, groups, answer, 0)
        a_own(t).start()

    for t in range(ticks):
        a_own(t).wait()
        for i in range(1, groups):
            a_out(t, i).wait()
            kv_out(t, i).wait_send()
            q_out(t, i).wait_send()
        for j in range(1, members):
            w_out(t, j).wait_send()
            for i in range(groups):
                relay(t, j, i).wait_send()

    @pl.when(block < blocks - 1)
    def _():
        pass_on().wait_send()


def shards(keys, values, queries, rates, counts, stagger, gate_in, up_in, down_in, entry_gate, entry_up, entry_down):
    ticks, rows = keys.shape[1:3]
    heads, size, width = gate_in.shape[1:]
    count = lax.axis_size("tok")
    blocks = lax.axis_size("block")
    groups = math.gcd(heads, count)
    members = count // groups
    own = heads // groups
    hid = groups * width
    edge = own * size
    room = -own % 16
    me = lax.axis_index("tok")
    group, member = me // members, me % members
    across = [[z * members + c for z in range(groups)] for c in range(members)]

    def exchange(x):
        return lax.all_to_all(x, "tok", 0, 0, axis_index_groups=across)

    def by_group(x):
        return x.reshape(ticks, rows, groups, -1).transpose(0, 2, 3, 1)

    scale = by_group(row_scale(rates[0], counts[0], stagger))
    scale = jnp.pad(scale, ((0, 0), (0, 0), (0, room), (0, 0)))
    pack = jnp.concatenate([by_group(keys[0]), by_group(values[0]), scale], axis=2)
    asked = by_group(queries[0])
    w = jnp.stack([gate_in[0], up_in[0], down_in[0]])
    w = w.reshape(3, groups, own, size, width).transpose(1, 0, 2, 3, 4)
    w = exchange(w).transpose(1, 2, 3, 0, 4).reshape(3, own, size, hid)
    entry = jnp.stack([entry_gate, entry_up, entry_down]).reshape(3, heads, size, groups, members, width)
    entry = lax.dynamic_slice_in_dim(entry, group * own, own, 1)
    entry = lax.dynamic_index_in_dim(entry, member, 4, keepdims=False).reshape(w.shape)

    dma = pltpu.SemaphoreType.DMA
    vmem = pl.BlockSpec(memory_space=pltpu.VMEM)
    answers, new = pl.pallas_call(
        functools.partial(kernel, groups, members, own, size, blocks),
        out_shape=(
            jax.ShapeDtypeStruct((ticks, groups, edge, rows), BF16),
            jax.ShapeDtypeStruct(w.shape, BF16),
        ),
        in_specs=[vmem] * 4,
        out_specs=(pl.BlockSpec(memory_space=pl.ANY), vmem),
        scratch_shapes=[
            pltpu.VMEM((ticks, members, groups, pack.shape[2], rows), BF16),
            pltpu.VMEM((ticks, groups, edge, rows), BF16),
            pltpu.VMEM((ticks, members, *w.shape), BF16),
            pltpu.VMEM(w.shape, BF16),
            pltpu.VMEM((ticks, groups, edge, rows), BF16),
            pltpu.VMEM(w.shape, F32),
            pltpu.VMEM((own, 2 * hid, size), BF16),
            pltpu.VMEM((own, hid, size), BF16),
            pltpu.VMEM((members, own, 2 * hid, size), BF16),
            dma((ticks, groups)), dma((ticks, groups)),
            dma((ticks, members, groups)), dma((ticks, members, groups)),
            dma((ticks, groups)), dma((ticks, groups)),
            dma((ticks, members)), dma((ticks, members)),
            dma((2,)),
            dma((ticks, groups)), dma((ticks, groups)),
            dma((3, ticks)),
        ],
        compiler_params=pltpu.CompilerParams(collective_id=0, has_side_effects=True),
        name="ttt",
    )(pack, asked, w, entry)
    answers = answers.transpose(0, 3, 1, 2).reshape(1, ticks, rows, heads * size)
    new = new.reshape(3, own, size, groups, width).transpose(3, 0, 1, 2, 4)
    new = exchange(new).transpose(1, 0, 2, 3, 4).reshape(3, 1, heads, size, width)
    return (answers, new[0], new[1], new[2])


def solution(mesh):
    tokens = P("block", None, "tok", None)
    hidden = P("block", None, None, "tok")
    return jax.shard_map(
        shards,
        mesh=mesh,
        in_specs=(tokens,) * 5 + (P(),) + (hidden,) * 3 + (P(),) * 3,
        out_specs=(tokens, hidden, hidden, hidden),
        check_vma=False,
    )
```

profile of v0, /device:TPU:0, one launch (start us, length us, event | category | flops | bytes accessed | tf_op | source)
XLA Modules:
  0.0 193.8 jit_solution(11334070586409467047)
XLA Ops:
  0.6 1.4 pad_maximum_fusion
  2.0 0.1 copy.54
  2.1 1.5 reshape.103
  3.6 6.3 %all-to-all-start = ((bf16[4,2,30720]{2,1,0:T(2,128)(2,1)}), bf16[4,2,30720]{2,1,0:T(2,128)(2,1)S(1)}, u32[]{:S(2)}, u32[]{:S(2)}) async-start(bf16[4,2,30720]{2,1,0:T(2,128)(2,1)} %reshape.103), calls=%async_computation | async-start | bytes 983040 | tf_op jit(solution)/shard_map/all_to_all | solution.py:282
  10.0 5.3 %stack.16 = bf16[1,20,64,4,2,64]{5,4,3,2,1,0:T(2,128)(2,1)S(1)} reshape(bf16[20,64,512]{2,1,0:T(8,128)(2,1)} %param.21) | data formatting | bytes 2621440 | tf_op jit(solution)/shard_map/stack | solution.py:294
  15.3 2.8 %copy.56 = bf16[1,20,64,4,2,64]{5,3,2,1,0,4:T(4,128)(2,1)} copy(bf16[1,20,64,4,2,64]{5,4,3,2,1,0:T(2,128)(2,1)S(1)} %stack.16) | data formatting | bytes 2621440 | tf_op jit(solution)/shard_map/stack | solution.py:294
  18.1 5.3 %stack.17 = bf16[1,20,64,4,2,64]{5,4,3,2,1,0:T(2,128)(2,1)S(1)} reshape(bf16[20,64,512]{2,1,0:T(8,128)(2,1)} %param.22) | data formatting | bytes 2621440 | tf_op jit(solution)/shard_map/stack | solution.py:294
  23.4 2.8 %copy.57 = bf16[1,20,64,4,2,64]{5,3,2,1,0,4:T(4,128)(2,1)} copy(bf16[1,20,64,4,2,64]{5,4,3,2,1,0:T(2,128)(2,1)S(1)} %stack.17) | data formatting | bytes 2621440 | tf_op jit(solution)/shard_map/stack | solution.py:294
  26.2 5.3 %stack.18 = bf16[1,20,64,4,2,64]{5,4,3,2,1,0:T(2,128)(2,1)S(1)} reshape(bf16[20,64,512]{2,1,0:T(8,128)(2,1)} %param.23) | data formatting | bytes 2621440 | tf_op jit(solution)/shard_map/stack | solution.py:294
  31.5 2.8 %copy.58 = bf16[1,20,64,4,2,64]{5,3,2,1,0,4:T(4,128)(2,1)} copy(bf16[1,20,64,4,2,64]{5,4,3,2,1,0:T(2,128)(2,1)S(1)} %stack.18) | data formatting | bytes 2621440 | tf_op jit(solution)/shard_map/stack | solution.py:294
  34.3 0.0 copy-start
  34.3 2.2 %fusion.3 = bf16[3,5,64,4,1,64]{5,3,2,1,0,4:T(4,128)(2,1)S(1)} fusion(s32[]{:T(128)S(6)} %select_n.42, s32[]{:T(128)S(6)} %select_n.45, bf16[1,20,64,4,2,64]{5,3,2,1,0,4:T(4,128)(2,1)} %copy.58, bf16[1,20,64,4,2,64]{5,3,2,1,0,4:T(4,128)(2,1)} %copy.57, bf16[1,20,64,4,2,64]{5,3,2,1,0,4:T(4,128)(2,1)} %copy.56), kind=kLoop, calls=%fused_computation.7 | loop fusion | flops 491520 | bytes 4423688 | tf_op jit(solution)/shard_map/stack | solution.py:294
  36.5 1.4 reshape.91.entry_ref
  37.9 0.0 copy-done
  37.9 0.0 copy-start.3
  37.9 0.0 copy-start.2
  37.9 0.6 copy.50
  38.5 0.0 copy-start.1
  38.5 1.6 copy.51
  40.1 0.0 copy-done.3
  40.1 0.1 sub.25
  40.2 0.5 broadcast.63
  40.7 0.0 copy-done.2
  40.7 0.7 reduce.3
  41.4 0.1 lt.37
  41.5 2.4 %copy.53 = bf16[1,2,256,1280]{2,3,1,0:T(8,128)(2,1)} copy(bf16[1,2,256,1280]{3,2,1,0:T(8,128)(2,1)} %param.14) | data formatting | bytes 2621440 | tf_op args[2]
  43.9 0.1 add_select_fusion
  44.0 0.0 copy-done.1
  44.0 0.1 fusion.5
  44.1 1.7 fusion.1.pack_ref
  45.8 0.0 all-to-all-done
  45.8 0.6 reshape.104
  46.4 0.8 copy.55
  47.2 1.4 reshape.90.w_ref
  48.7 121.9 %ttt.1 = (bf16[2,4,320,256]{3,2,1,0:T(8,128)(2,1)}, bf16[3,5,64,256]{3,2,1,0:T(8,128)(2,1)}) custom-call(bf16[2,4,656,256]{3,2,1,0:T(8,128)(2,1)} %fusion.1.pack_ref, bf16[2,4,320,256]{3,2,1,0:T(8,128)(2,1)} %bitcast.30, bf16[3,5,64,256]{3,2,1,0:T(8,128)(2,1)} %reshape.90.w_ref, bf16[3,5,64,256]{3,2,1,0:T(8,128)(2,1)} %reshape.91.entry_ref), custom_call_target="tpu_custom_call" | custom-call | tf_op jit(solution)/shard_map/ttt/pallas_call | solution.py:300
  170.6 2.0 %reshape.93 = bf16[3,5,64,4,64]{4,3,2,1,0:T(4,128)(2,1)S(1)} reshape(bf16[3,5,64,256]{3,2,1,0:T(8,128)(2,1)} %get-tuple-element.7) | data formatting | bytes 983040 | tf_op jit(solution)/shard_map/reshape | solution.py:330
  172.6 0.2 copy.63
  172.8 1.5 reshape.105
  174.3 3.5 %all-to-all-start.1 = ((bf16[4,2,30720]{2,1,0:T(2,128)(2,1)}), bf16[4,2,30720]{2,1,0:T(2,128)(2,1)S(1)}, u32[]{:S(2)}, u32[]{:S(2)}) async-start(bf16[4,2,30720]{2,1,0:T(2,128)(2,1)} %reshape.105), calls=%async_computation.1 | async-start | bytes 983040 | tf_op jit(solution)/shard_map/all_to_all | solution.py:282
  177.8 2.4 %copy.60 = bf16[1,2,256,1280]{3,2,1,0:T(8,128)(2,1)} copy(bf16[1,2,256,1280]{2,3,1,0:T(8,128)(2,1)} %bitcast.37) | data formatting | bytes 2621440
  180.2 12.0 %all-to-all-done.1 = bf16[4,2,30720]{2,1,0:T(2,128)(2,1)S(1)} async-done(((bf16[4,2,30720]{2,1,0:T(2,128)(2,1)}), bf16[4,2,30720]{2,1,0:T(2,128)(2,1)S(1)}, u32[]{:S(2)}, u32[]{:S(2)}) %all-to-all-start.1) | async-done | bytes 491552 | tf_op jit(solution)/shard_map/all_to_all | solution.py:282
  192.2 0.6 reshape.106
  192.8 1.0 fusion.9
Async XLA Ops:
  3.6 42.1 %all-to-all-start = ((bf16[4,2,30720]{2,1,0:T(2,128)(2,1)}), bf16[4,2,30720]{2,1,0:T(2,128)(2,1)S(1)}, u32[]{:S(2)}, u32[]{:S(2)}) async-start(bf16[4,2,30720]{2,1,0:T(2,128)(2,1)} %reshape.103), calls=%async_computation | async-start | bytes 983040 | tf_op jit(solution)/shard_map/all_to_all | solution.py:282
  34.3 3.6 %copy-start = (bf16[1,2,256,1280]{3,2,1,0:T(8,128)(2,1)S(1)}, bf16[1,2,256,1280]{3,2,1,0:T(8,128)(2,1)}, u32[]{:S(2)}) copy-start(bf16[1,2,256,1280]{3,2,1,0:T(8,128)(2,1)} %param.12) | copy-start | bytes 3932164
  37.9 2.2 %copy-start.3 = (s32[20]{0:T(128)S(1)}, s32[20]{0:T(128)}, u32[]{:S(2)}) copy-start(s32[20]{0:T(128)} %param.17) | copy-start | bytes 244
  37.9 2.8 %copy-start.2 = (s32[1,2,1,20]{3,2,1,0:T(1,128)S(1)}, s32[1,2,1,20]{3,2,1,0:T(1,128)}, u32[]{:S(2)}) copy-start(s32[1,2,1,20]{3,2,1,0:T(1,128)} %param.16) | copy-start | bytes 484
  38.5 5.5 %copy-start.1 = (bf16[1,2,256,20]{2,1,3,0:T(2,128)(2,1)S(1)}, bf16[1,2,256,20]{2,1,3,0:T(2,128)(2,1)}, u32[]{:S(2)}) copy-start(bf16[1,2,256,20]{2,1,3,0:T(2,128)(2,1)} %param.15) | copy-start | bytes 61444
  174.3 17.9 %all-to-all-start.1 = ((bf16[4,2,30720]{2,1,0:T(2,128)(2,1)}), bf16[4,2,30720]{2,1,0:T(2,128)(2,1)S(1)}, u32[]{:S(2)}, u32[]{:S(2)}) async-start(bf16[4,2,30720]{2,1,0:T(2,128)(2,1)} %reshape.105), calls=%async_computation.1 | async-start | bytes 983040 | tf_op jit(solution)/shard_map/all_to_all | solution.py:282
where the time goes:
time: 194 us
  Pallas kernels  122 us (63%)
  local copies, waits for them, and re-layouts  43.1 us (22%)
  waiting for transfers between devices  12 us (6%)
  starting transfers between devices  9.81 us (5%)
  other arithmetic  6.16 us (3%)
    pallas_call x1, Pallas kernels, shards(): pl.pallas_call(functools.partial(kernel, groups, members, own, size, bloc...  122 us
    another operation x6, local copies, waits for them, and re-layouts, shards(): jnp.stack([entry_gate, entry_up, entry_down])  24.3 us
    all_to_all x2, waiting for transfers between devices, exchange(): return lax.all_to_all(x, 'tok', 0, 0, axis_index_groups=across)  12 us
    unnamed x17, local copies, waits for them, and re-layouts  11.8 us
    all_to_all x2, starting transfers between devices, exchange(): return lax.all_to_all(x, 'tok', 0, 0, axis_index_groups=across)  9.81 us
  transfers between devices with their start and end apart: 2, of which 1 were waited for; matrix products, arithmetic and copies ran while one was open for 20% of the time, Pallas kernels for 0%

commit v1 on v0

--- a/solution.py
+++ b/solution.py
@@ -39,14 +39,15 @@
 
 def kernel(
     groups, members, own, size, blocks,
-    pack_ref, ask_ref, w_ref, entry_ref, ans_ref, wout_ref,
-    kv, qs, full, carry, reply, acc, gut, wt, gut_all,
+    pack_ref, ask_ref, pair_ref, down_ref, entry0, entry1, entry2, ans_ref, pair_out, down_out,
+    kv, qs, first, pairs, downs, pair_back, down_back, entry, full, carry, reply, acc, gut, wt, gut_all,
     kv_send, kv_recv, relay_send, relay_recv, q_send, q_recv,
-    w_send, w_recv, carry_sem, a_send, a_recv, local,
+    g_send, g_recv, d_send, d_recv, gb_send, gb_recv, db_send, db_recv, entry_sem, w_send, w_recv, carry_sem, a_send, a_recv, local,
 ):
     ticks = pack_ref.shape[0]
     edge = own * size
-    hid = w_ref.shape[3]
+    hid = first.shape[3]
+    width = hid // groups
     block = lax.axis_index("block")
     me = lax.axis_index("tok")
     z = me // members
@@ -110,6 +111,34 @@
     def pass_on():
         return remote(full.at[0, c], carry, carry_sem.at[0], carry_sem.at[1], (lax.rem(block + 1, blocks), me))
 
+    def pair_put(i):
+        return remote(pair_ref.at[ahead(i)], pairs.at[z], g_send.at[i], g_recv.at[i], at(ahead(i), c))
+
+    def down_put(i):
+        return remote(down_ref.at[ahead(i)], downs.at[z], d_send.at[i], d_recv.at[i], at(ahead(i), c))
+
+    def pair_give(i):
+        return remote(pair_back.at[ahead(i)], pair_out.at[z], gb_send.at[i], gb_recv.at[i], at(ahead(i), c))
+
+    def down_give(i):
+        return remote(down_back.at[ahead(i)], down_out.at[z], db_send.at[i], db_recv.at[i], at(ahead(i), c))
+
+    def w_own():
+        return (
+            pltpu.make_async_copy(pair_ref.at[z], pairs.at[z], local.at[3, 0]),
+            pltpu.make_async_copy(down_ref.at[z], downs.at[z], local.at[3, 1]),
+        )
+
+    def w_back():
+        return (
+            pltpu.make_async_copy(pair_back.at[z], pair_out.at[z], local.at[4, 0]),
+            pltpu.make_async_copy(down_back.at[z], down_out.at[z], local.at[4, 1]),
+        )
+
+    def entry_own(p):
+        whole = (entry0, entry1, entry2)[p]
+        return pltpu.make_async_copy(whole.at[pl.ds(z * own, own)], entry.at[p], entry_sem.at[p])
+
     def kv_own(t):
         return pltpu.make_async_copy(pack_ref.at[t, z], kv.at[t, c, z], local.at[0, t])
 
@@ -120,18 +149,42 @@
         return pltpu.make_async_copy(reply.at[t, z], ans_ref.at[t, z], local.at[2, t])
 
     for i in range(1, groups):
+        pair_put(i).start()
+        down_put(i).start()
+    for i in range(1, groups):
         kv_out(0, i).start()
+    for copy in w_own():
+        copy.start()
     for t in range(ticks):
         kv_own(t).start()
         q_own(t).start()
+    for p in range(3):
+        entry_own(p).start()
+    for copy in w_own():
+        copy.wait()
+    for i in range(1, groups):
+        pair_put(i).wait_recv()
+        down_put(i).wait_recv()
+    for h in range(own):
+        for p, (held, low) in enumerate(((pairs, 0), (pairs, width), (downs, 0))):
+            parts = [held[zz, h, :, low : low + width] for zz in range(groups)]
+            first[p, h] = jnp.concatenate(parts, axis=1)
 
     for t in range(ticks):
-        weights = w_ref if t == 0 else carry
+        weights = first if t == 0 else carry
         if t > 0:
 
-            @pl.when(block == 0)
-            def _():
-                carry[...] = entry_ref[...]
+            for p in range(3):
+                entry_own(p).wait()
+            for s in range(members):
+
+                @pl.when((block == 0) & (c == s))
+                def _(s=s):
+                    for p in range(3):
+                        for h in range(own):
+                            lows = [(zz * members + s) * width for zz in range(groups)]
+                            parts = [entry[p, h, :, low : low + width] for low in lows]
+                            carry[p, h] = jnp.concatenate(parts, axis=1)
 
             @pl.when(block > 0)
             def _():
@@ -207,7 +260,17 @@
                 pass_on().start()
 
         else:
-            wout_ref[...] = full[t, c]
+            for zz in range(groups):
+                lanes = slice(zz * width, (zz + 1) * width)
+                for h in range(own):
+                    pair_back[zz, h, :, :width] = full[t, c, 0, h, :, lanes]
+                    pair_back[zz, h, :, width:] = full[t, c, 1, h, :, lanes]
+                    down_back[zz, h] = full[t, c, 2, h, :, lanes]
+            for i in range(1, groups):
+                pair_give(i).start()
+                down_give(i).start()
+            for copy in w_back():
+                copy.start()
         for j in range(1, members):
             w_out(t, j).wait_recv()
 
@@ -257,6 +320,14 @@
             w_out(t, j).wait_send()
             for i in range(groups):
                 relay(t, j, i).wait_send()
+
+    for i in range(1, groups):
+        pair_put(i).wait_send()
+        down_put(i).wait_send()
+        pair_give(i).wait()
+        down_give(i).wait()
+    for copy in w_back():
+        copy.wait()
 
     @pl.when(block < blocks - 1)
     def _():
@@ -274,13 +345,6 @@
     hid = groups * width
     edge = own * size
     room = -own % 16
-    me = lax.axis_index("tok")
-    group, member = me // members, me % members
-    across = [[z * members + c for z in range(groups)] for c in range(members)]
-
-    def exchange(x):
-        return lax.all_to_all(x, "tok", 0, 0, axis_index_groups=across)
-
     def by_group(x):
         return x.reshape(ticks, rows, groups, -1).transpose(0, 2, 3, 1)
 
@@ -288,48 +352,54 @@
     scale = jnp.pad(scale, ((0, 0), (0, 0), (0, room), (0, 0)))
     pack = jnp.concatenate([by_group(keys[0]), by_group(values[0]), scale], axis=2)
     asked = by_group(queries[0])
-    w = jnp.stack([gate_in[0], up_in[0], down_in[0]])
-    w = w.reshape(3, groups, own, size, width).transpose(1, 0, 2, 3, 4)
-    w = exchange(w).transpose(1, 2, 3, 0, 4).reshape(3, own, size, hid)
-    entry = jnp.stack([entry_gate, entry_up, entry_down]).reshape(3, heads, size, groups, members, width)
-    entry = lax.dynamic_slice_in_dim(entry, group * own, own, 1)
-    entry = lax.dynamic_index_in_dim(entry, member, 4, keepdims=False).reshape(w.shape)
+    pair = jnp.concatenate([gate_in[0], up_in[0]], axis=2).reshape(groups, own, size, 2 * width)
+    down = down_in[0].reshape(groups, own, size, width)
+    shape = (3, own, size, hid)
 
     dma = pltpu.SemaphoreType.DMA
     vmem = pl.BlockSpec(memory_space=pltpu.VMEM)
-    answers, new = pl.pallas_call(
+    hbm = pl.BlockSpec(memory_space=pl.ANY)
+    answers, pair, down = pl.pallas_call(
         functools.partial(kernel, groups, members, own, size, blocks),
         out_shape=(
             jax.ShapeDtypeStruct((ticks, groups, edge, rows), BF16),
-            jax.ShapeDtypeStruct(w.shape, BF16),
+            jax.ShapeDtypeStruct(pair.shape, BF16),
+            jax.ShapeDtypeStruct(down.shape, BF16),
         ),
-        in_specs=[vmem] * 4,
-        out_specs=(pl.BlockSpec(memory_space=pl.ANY), vmem),
+        in_specs=[vmem] * 4 + [hbm] * 3,
+        out_specs=(hbm, hbm, hbm),
         scratch_shapes=[
             pltpu.VMEM((ticks, members, groups, pack.shape[2], rows), BF16),
             pltpu.VMEM((ticks, groups, edge, rows), BF16),
-            pltpu.VMEM((ticks, members, *w.shape), BF16),
-            pltpu.VMEM(w.shape, BF16),
+            pltpu.VMEM(shape, BF16),
+            pltpu.VMEM(pair.shape, BF16),
+            pltpu.VMEM(down.shape, BF16),
+            pltpu.VMEM(pair.shape, BF16),
+            pltpu.VMEM(down.shape, BF16),
+            pltpu.VMEM((3, own, size, entry_gate.shape[2]), BF16),
+            pltpu.VMEM((ticks, members, *shape), BF16),
+            pltpu.VMEM(shape, BF16),
             pltpu.VMEM((ticks, groups, edge, rows), BF16),
-            pltpu.VMEM(w.shape, F32),
+            pltpu.VMEM(shape, F32),
             pltpu.VMEM((own, 2 * hid, size), BF16),
             pltpu.VMEM((own, hid, size), BF16),
             pltpu.VMEM((members, own, 2 * hid, size), BF16),
             dma((ticks, groups)), dma((ticks, groups)),
             dma((ticks, members, groups)), dma((ticks, members, groups)),
             dma((ticks, groups)), dma((ticks, groups)),
+            *[dma((groups,)) for _ in range(8)],
+            dma((3,)),
             dma((ticks, members)), dma((ticks, members)),
             dma((2,)),
             dma((ticks, groups)), dma((ticks, groups)),
-            dma((3, ticks)),
+            dma((5, max(2, ticks))),
         ],
         compiler_params=pltpu.CompilerParams(collective_id=0, has_side_effects=True),
         name="ttt",
-    )(pack, asked, w, entry)
+    )(pack, asked, pair, down, entry_gate, entry_up, entry_down)
     answers = answers.transpose(0, 3, 1, 2).reshape(1, ticks, rows, heads * size)
-    new = new.reshape(3, own, size, groups, width).transpose(3, 0, 1, 2, 4)
-    new = exchange(new).transpose(1, 0, 2, 3, 4).reshape(3, 1, heads, size, width)
-    return (answers, new[0], new[1], new[2])
+    pair = pair.reshape(1, heads, size, 2 * width)
+    return (answers, pair[..., :width], pair[..., width:], down.reshape(1, heads, size, width))
 
 
 def solution(mesh):

time: 194 us -> 176 us (0.907)
  Pallas kernels: 122 us -> 158 us
  local copies, waits for them, and re-layouts: 43.1 us -> 11.1 us
  waiting for transfers between devices: 12 us -> 0 us
  starting transfers between devices: 9.81 us -> 0 us
    pallas_call x1, Pallas kernels: 122 us -> 158 us  [shards(): pl.pallas_call(functools.partial(kernel, groups, members, own, size, bloc...]
    another operation x6 -> x0, local copies, waits for them, and re-layouts: 24.3 us -> none  [shards(): jnp.stack([entry_gate, entry_up, entry_down])]
    all_to_all x2 -> x0, waiting for transfers between devices: 12 us -> none  [exchange(): return lax.all_to_all(x, 'tok', 0, 0, axis_index_groups=across)]
    all_to_all x2 -> x0, starting transfers between devices: 9.81 us -> none  [exchange(): return lax.all_to_all(x, 'tok', 0, 0, axis_index_groups=across)]
    reshape x4 -> x0, local copies, waits for them, and re-layouts: 5.03 us -> none  [the longest x2 2.2 us: shards(): new = new.reshape(3, own, size, groups, width).transpose(3, 0, 1, 2, 4)]
    another operation x2 -> x0, other arithmetic: 3.62 us -> none  [the longest x1 2.21 us: shards(): jnp.stack([entry_gate, entry_up, entry_down])]
    unnamed x17 -> x10, local copies, waits for them, and re-layouts: 11.8 us -> 9.33 us
    concatenate x0 -> x1, other arithmetic: none -> 1.98 us  [shards(): jnp.concatenate([gate_in[0], up_in[0]], axis=2)]
  transfers between devices with their start and end apart: 2 -> 0, of which waited for: 1 -> 0; matrix products, arithmetic and copies ran while one was open for 20% -> 0% of each run, Pallas kernels for 0% -> 0%
where the time goes in v1:
time: 176 us
  Pallas kernels  158 us (90%)
  local copies, waits for them, and re-layouts  11.1 us (6%)
  other arithmetic  5.92 us (3%)
    pallas_call x1, Pallas kernels, shards(): pl.pallas_call(functools.partial(kernel, groups, members, own, size, bloc...  158 us
    unnamed x10, local copies, waits for them, and re-layouts  9.33 us

profile of v1, /device:TPU:0, one launch (start us, length us, event | category | flops | bytes accessed | tf_op | source)
XLA Modules:
  0.0 176.0 jit_solution(15643042033221657879)
XLA Ops:
  0.6 0.5 broadcast.61
  1.1 1.3 reduce.3
  2.5 0.7 sub.21
  3.2 0.1 lt.24
  3.3 0.1 add_select_fusion
  3.4 0.8 fusion.3
  4.2 2.0 %pad_maximum_fusion.pair_ref = bf16[4,5,64,128]{3,2,1,0:T(8,128)(2,1)} fusion(bf16[4,5,64,64]{3,2,1,0:T(8,128)(2,1)} %bitcast.27, bf16[4,5,64,64]{3,2,1,0:T(8,128)(2,1)} %bitcast.28), kind=kLoop, calls=%fused_computation.3 | loop fusion | flops 655360 | bytes 655360 | tf_op jit(solution)/shard_map/concatenate | solution.py:355
  6.2 1.6 copy.21
  7.8 1.6 copy.22
  9.4 1.7 fusion.1.pack_ref
  11.1 2.4 %copy.24 = bf16[1,2,256,1280]{2,3,1,0:T(8,128)(2,1)} copy(bf16[1,2,256,1280]{3,2,1,0:T(8,128)(2,1)} %param.14) | data formatting | bytes 2621440 | tf_op args[2]
  13.5 158.2 %ttt.1 = (bf16[2,4,320,256]{3,2,1,0:T(8,128)(2,1)}, bf16[4,5,64,128]{3,2,1,0:T(8,128)(2,1)}, bf16[4,5,64,64]{3,2,1,0:T(8,128)(2,1)}) custom-call(bf16[2,4,656,256]{3,2,1,0:T(8,128)(2,1)} %fusion.1.pack_ref, bf16[2,4,320,256]{3,2,1,0:T(8,128)(2,1)} %bitcast.22, bf16[4,5,64,128]{3,2,1,0:T(8,128)(2,1)} %pad_maximum_fusion.pair_ref, ...), custom_call_target="tpu_custom_call" | custom-call | tf_op jit(solution)/shard_map/ttt/pallas_call | solution.py:362
  171.8 0.0 copy-start
  171.8 0.0 copy-start.1
  171.8 2.5 %copy.25 = bf16[1,2,256,1280]{3,2,1,0:T(8,128)(2,1)} copy(bf16[1,2,256,1280]{2,3,1,0:T(8,128)(2,1)} %bitcast.23) | data formatting | bytes 2621440
  174.3 0.0 copy-done
  174.3 1.0 fusion.7
  175.2 0.0 copy-done.1
  175.2 0.7 copy.28
Async XLA Ops:
  171.8 2.5 %copy-start = (bf16[4,5,64,128]{3,2,1,0:T(8,128)(2,1)S(1)}, bf16[4,5,64,128]{3,2,1,0:T(8,128)(2,1)}, u32[]{:S(2)}) copy-start(bf16[4,5,64,128]{3,2,1,0:T(8,128)(2,1)} %get-tuple-element.8) | copy-start | bytes 983044
  171.8 3.5 %copy-start.1 = (bf16[4,5,64,64]{3,2,1,0:T(8,128)(2,1)S(1)}, bf16[4,5,64,64]{3,2,1,0:T(8,128)(2,1)}, u32[]{:S(2)}) copy-start(bf16[4,5,64,64]{3,2,1,0:T(8,128)(2,1)} %get-tuple-element.9) | copy-start | bytes 491524

commit v2 on v1

--- a/solution.py
+++ b/solution.py
@@ -39,15 +39,16 @@
 
 def kernel(
     groups, members, own, size, blocks,
-    pack_ref, ask_ref, pair_ref, down_ref, entry0, entry1, entry2, ans_ref, pair_out, down_out,
-    kv, qs, first, pairs, downs, pair_back, down_back, entry, full, carry, reply, acc, gut, wt, gut_all,
+    pack_ref, ask_ref, pair_ref, entry0, entry1, entry2, ans_ref, pair_out,
+    kv, qs, first, pairs, pair_back, entry, full, carry, reply, acc, gut, wt, gut_all,
     kv_send, kv_recv, relay_send, relay_recv, q_send, q_recv,
-    g_send, g_recv, d_send, d_recv, gb_send, gb_recv, db_send, db_recv, entry_sem, w_send, w_recv, carry_sem, a_send, a_recv, local,
+    g_send, g_recv, gb_send, gb_recv, entry_sem, w_send, w_recv, carry_sem, a_send, a_recv, local,
 ):
     ticks = pack_ref.shape[0]
     edge = own * size
     hid = first.shape[3]
     width = hid // groups
+    half = pairs.shape[1]
     block = lax.axis_index("block")
     me = lax.axis_index("tok")
     z = me // members
@@ -114,26 +115,14 @@
     def pair_put(i):
         return remote(pair_ref.at[ahead(i)], pairs.at[z], g_send.at[i], g_recv.at[i], at(ahead(i), c))
 
-    def down_put(i):
-        return remote(down_ref.at[ahead(i)], downs.at[z], d_send.at[i], d_recv.at[i], at(ahead(i), c))
-
     def pair_give(i):
         return remote(pair_back.at[ahead(i)], pair_out.at[z], gb_send.at[i], gb_recv.at[i], at(ahead(i), c))
 
-    def down_give(i):
-        return remote(down_back.at[ahead(i)], down_out.at[z], db_send.at[i], db_recv.at[i], at(ahead(i), c))
-
     def w_own():
-        return (
-            pltpu.make_async_copy(pair_ref.at[z], pairs.at[z], local.at[3, 0]),
-            pltpu.make_async_copy(down_ref.at[z], downs.at[z], local.at[3, 1]),
-        )
+        return pltpu.make_async_copy(pair_ref.at[z], pairs.at[z], local.at[3, 0])
 
     def w_back():
-        return (
-            pltpu.make_async_copy(pair_back.at[z], pair_out.at[z], local.at[4, 0]),
-            pltpu.make_async_copy(down_back.at[z], down_out.at[z], local.at[4, 1]),
-        )
+        return pltpu.make_async_copy(pair_back.at[z], pair_out.at[z], local.at[4, 0])
 
     def entry_own(p):
         whole = (entry0, entry1, entry2)[p]
@@ -150,24 +139,21 @@
 
     for i in range(1, groups):
         pair_put(i).start()
-        down_put(i).start()
     for i in range(1, groups):
         kv_out(0, i).start()
-    for copy in w_own():
-        copy.start()
+    w_own().start()
     for t in range(ticks):
         kv_own(t).start()
         q_own(t).start()
     for p in range(3):
         entry_own(p).start()
-    for copy in w_own():
-        copy.wait()
+    w_own().wait()
     for i in range(1, groups):
         pair_put(i).wait_recv()
-        down_put(i).wait_recv()
     for h in range(own):
-        for p, (held, low) in enumerate(((pairs, 0), (pairs, width), (downs, 0))):
-            parts = [held[zz, h, :, low : low + width] for zz in range(groups)]
+        for p in range(3):
+            spot, side = (p * own + h) % half, (p * own + h) // half * width
+            parts = [pairs[zz, spot, :, side : side + width] for zz in range(groups)]
             first[p, h] = jnp.concatenate(parts, axis=1)
 
     for t in range(ticks):
@@ -262,15 +248,16 @@
         else:
             for zz in range(groups):
                 lanes = slice(zz * width, (zz + 1) * width)
-                for h in range(own):
-                    pair_back[zz, h, :, :width] = full[t, c, 0, h, :, lanes]
-                    pair_back[zz, h, :, width:] = full[t, c, 1, h, :, lanes]
-                    down_back[zz, h] = full[t, c, 2, h, :, lanes]
+                for n in range(2 * half):
+                    spot, side = n % half, n // half * width
+                    if n < 3 * own:
+                        piece = full[t, c, n // own, n % own, :, lanes]
+                    else:
+                        piece = jnp.zeros((size, width), BF16)
+                    pair_back[zz, spot, :, side : side + width] = piece
             for i in range(1, groups):
                 pair_give(i).start()
-                down_give(i).start()
-            for copy in w_back():
-                copy.start()
+            w_back().start()
         for j in range(1, members):
             w_out(t, j).wait_recv()
 
@@ -323,11 +310,8 @@
 
     for i in range(1, groups):
         pair_put(i).wait_send()
-        down_put(i).wait_send()
         pair_give(i).wait()
-        down_give(i).wait()
-    for copy in w_back():
-        copy.wait()
+    w_back().wait()
 
     @pl.when(block < blocks - 1)
     def _():
@@ -352,30 +336,30 @@
     scale = jnp.pad(scale, ((0, 0), (0, 0), (0, room), (0, 0)))
     pack = jnp.concatenate([by_group(keys[0]), by_group(values[0]), scale], axis=2)
     asked = by_group(queries[0])
-    pair = jnp.concatenate([gate_in[0], up_in[0]], axis=2).reshape(groups, own, size, 2 * width)
-    down = down_in[0].reshape(groups, own, size, width)
+    half = (3 * own + 1) // 2
+    slots = jnp.stack([gate_in[0], up_in[0], down_in[0]]).reshape(3, groups, own, size, width)
+    slots = slots.transpose(1, 0, 2, 3, 4).reshape(groups, 3 * own, size, width)
+    slots = jnp.pad(slots, ((0, 0), (0, 2 * half - 3 * own), (0, 0), (0, 0)))
+    pair = jnp.concatenate([slots[:, :half], slots[:, half:]], axis=3)
     shape = (3, own, size, hid)
 
     dma = pltpu.SemaphoreType.DMA
     vmem = pl.BlockSpec(memory_space=pltpu.VMEM)
     hbm = pl.BlockSpec(memory_space=pl.ANY)
-    answers, pair, down = pl.pallas_call(
+    answers, pair = pl.pallas_call(
         functools.partial(kernel, groups, members, own, size, blocks),
         out_shape=(
             jax.ShapeDtypeStruct((ticks, groups, edge, rows), BF16),
             jax.ShapeDtypeStruct(pair.shape, BF16),
-            jax.ShapeDtypeStruct(down.shape, BF16),
         ),
-        in_specs=[vmem] * 4 + [hbm] * 3,
-        out_specs=(hbm, hbm, hbm),
+        in_specs=[vmem] * 3 + [hbm] * 3,
+        out_specs=(hbm, hbm),
         scratch_shapes=[
             pltpu.VMEM((ticks, members, groups, pack.shape[2], rows), BF16),
             pltpu.VMEM((ticks, groups, edge, rows), BF16),
             pltpu.VMEM(shape, BF16),
             pltpu.VMEM(pair.shape, BF16),
-            pltpu.VMEM(down.shape, BF16),
             pltpu.VMEM(pair.shape, BF16),
-            pltpu.VMEM(down.shape, BF16),
             pltpu.VMEM((3, own, size, entry_gate.shape[2]), BF16),
             pltpu.VMEM((ticks, members, *shape), BF16),
             pltpu.VMEM(shape, BF16),
@@ -387,7 +371,7 @@
             dma((ticks, groups)), dma((ticks, groups)),
             dma((ticks, members, groups)), dma((ticks, members, groups)),
             dma((ticks, groups)), dma((ticks, groups)),
-            *[dma((groups,)) for _ in range(8)],
+            *[dma((groups,)) for _ in range(4)],
             dma((3,)),
             dma((ticks, members)), dma((ticks, members)),
             dma((2,)),
@@ -396,10 +380,11 @@
         ],
         compiler_params=pltpu.CompilerParams(collective_id=0, has_side_effects=True),
         name="ttt",
-    )(pack, asked, pair, down, entry_gate, entry_up, entry_down)
+    )(pack, asked, pair, entry_gate, entry_up, entry_down)
     answers = answers.transpose(0, 3, 1, 2).reshape(1, ticks, rows, heads * size)
-    pair = pair.reshape(1, heads, size, 2 * width)
-    return (answers, pair[..., :width], pair[..., width:], down.reshape(1, heads, size, width))
+    slots = jnp.concatenate([pair[..., :width], pair[..., width:]], axis=1)[:, : 3 * own]
+    new = slots.reshape(groups, 3, own, size, width)
+    return (answers, *(new[:, p].reshape(1, heads, size, width) for p in range(3)))
 
 
 def solution(mesh):

time: 176 us -> 169 us (0.960)
  Pallas kernels: 158 us -> 152 us
    pallas_call x1, Pallas kernels: 158 us -> 152 us  [shards(): pl.pallas_call(functools.partial(kernel, groups, members, own, size, bloc...]
    unnamed x10 -> x9, local copies, waits for them, and re-layouts: 9.33 us -> 7.62 us
where the time goes in v2:
time: 169 us
  Pallas kernels  152 us (90%)
  local copies, waits for them, and re-layouts  9.87 us (6%)
  other arithmetic  6.65 us (4%)
    pallas_call x1, Pallas kernels, shards(): pl.pallas_call(functools.partial(kernel, groups, members, own, size, bloc...  152 us
    unnamed x9, local copies, waits for them, and re-layouts  7.62 us

profile of v2, /device:TPU:0, one launch (start us, length us, event | category | flops | bytes accessed | tf_op | source)
XLA Modules:
  0.0 169.0 jit_solution(8092172768332494481)
XLA Ops:
  0.6 0.5 broadcast.63
  1.1 1.3 reduce.3
  2.5 0.7 sub.21
  3.2 0.1 lt.24
  3.3 0.1 add_select_fusion
  3.4 0.8 fusion.3
  4.2 1.4 pad_maximum_fusion.1
  5.6 0.0 copy-start.1
  5.6 0.1 copy.26
  5.7 0.2 fusion.8
  5.9 1.1 pad_maximum_fusion.2.pair_ref
  7.0 0.0 copy-done.1
  7.0 0.6 copy.22
  7.6 1.6 copy.23
  9.2 1.7 %fusion.1.pack_ref = bf16[2,4,656,256]{3,2,1,0:T(8,128)(2,1)} fusion(bf16[2,4,5,256]{3,2,1,0:T(8,128)(2,1)S(1)} %fusion.3, bf16[2,4,320,256]{3,2,1,0:T(8,128)(2,1)S(1)} %bitcast.25, bf16[2,4,320,256]{3,2,1,0:T(8,128)(2,1)S(1)} %bitcast.24), kind=kLoop, calls=%fused_computation.2 | loop fusion | flops 10747904 | bytes 5328896 | tf_op jit(solution)/shard_map/concatenate | solution.py:337
  10.9 2.4 %copy.25 = bf16[1,2,256,1280]{2,3,1,0:T(8,128)(2,1)} copy(bf16[1,2,256,1280]{3,2,1,0:T(8,128)(2,1)} %param.14) | data formatting | bytes 2621440 | tf_op args[2]
  13.3 151.7 %ttt.1 = (bf16[2,4,320,256]{3,2,1,0:T(8,128)(2,1)}, bf16[4,8,64,128]{3,2,1,0:T(8,128)(2,1)}) custom-call(bf16[2,4,656,256]{3,2,1,0:T(8,128)(2,1)} %fusion.1.pack_ref, bf16[2,4,320,256]{3,2,1,0:T(8,128)(2,1)} %bitcast.26, bf16[4,8,64,128]{3,2,1,0:T(8,128)(2,1)} %pad_maximum_fusion.2.pair_ref, bf16[20,64,512]{2,1,0:T(8,128)(2,1)} %entry0.1, ...), custom_call_target="tpu_custom_call" | custom-call | tf_op jit(solution)/shard_map/ttt/pallas_call | solution.py:349
  165.0 0.0 copy-start
  165.0 2.5 %copy.27 = bf16[1,2,256,1280]{3,2,1,0:T(8,128)(2,1)} copy(bf16[1,2,256,1280]{2,3,1,0:T(8,128)(2,1)} %bitcast.29) | data formatting | bytes 2621440
  167.5 0.0 copy-done
  167.5 0.3 fusion.9
  167.8 0.2 pad_maximum_fusion
  168.0 1.0 fusion.7
Async XLA Ops:
  5.6 1.3 copy-start.1
  165.0 2.5 %copy-start = (bf16[4,8,64,128]{3,2,1,0:T(8,128)(2,1)S(1)}, bf16[4,8,64,128]{3,2,1,0:T(8,128)(2,1)}, u32[]{:S(2)}) copy-start(bf16[4,8,64,128]{3,2,1,0:T(8,128)(2,1)} %get-tuple-element.7) | copy-start | bytes 1572868
